TPU v7x, 32 devices: a whole 2x2x4 slice. The times are simulated.
32 devices in a mesh: blk: 8 (over z, y), head: 4 (over x, core).
Axes of the slice: x: 2, y: 2, z: 4, core: 2. Of those that a mesh axis runs over, the one named last changes fastest.
Arguments:
- queries: bfloat16 [4096, 1024], P('blk', 'head'), may hold values from -170 to 170
- key_rows: bfloat16 [4096, 1024], P('blk', 'head'), may hold values from -9 to 9
- values: bfloat16 [4096, 1024], P('blk', 'head'), may hold values from -48 to 48
- text_keys: bfloat16 [308, 1024], P(None, 'head'), may hold values from -9 to 9
- text_values: bfloat16 [308, 1024], P(None, 'head'), may hold values from -48 to 48
- block_image: int32 [32], replicated, may hold values from 0 to 1, as said below
- gate_image: float32 [2, 1536], replicated, may hold values from 0.5 to 2
- residual: bfloat16 [4096, 1536], P(('blk', 'head')), may hold values from -6 to 6
- w_out: bfloat16 [1024, 1536], P('head'), may hold values from -0.1875 to 0.1875
Outputs:
- stream_out: bfloat16 [4096, 1536], P(('blk', 'head'))
Inputs may be any that keep to these rules, and one draw needn't show every extreme that they name: `block_image`: each image number 0 to 1 names 8 to 24 of the entries, some image exactly 24 and some exactly 8; the blocks of an image lie anywhere in the array.
All inputs are finite; a program needn't handle non-finite values.
Results may differ from a plain program's by a relative error of at most 0.014.
Values may be sent and summed in bfloat16 or wider, within the bound.
No kernel may reach another device: no remote copies, remote signals or barrier semaphores. Data moves between devices by JAX's collectives and lax.ppermute only.
A program may use at most 64 MiB of HBM per device.

v0:
```python
import math

import jax
import jax.numpy as jnp
from jax import lax
from jax.sharding import PartitionSpec as P

HD = 64
TEXT = 154
BS = 128


neg_large = -1e30


def absorb(running, query_three, query_image, key_slab, value_slab, key_image):
    best, total, accum = running
    heads = query_three.shape[1]
    width = query_three.shape[2]
    key_three = key_slab.reshape(key_slab.shape[0], heads, width)
    value_three = value_slab.reshape(value_slab.shape[0], heads, width)
    scores = jnp.einsum("qhd,khd->hqk", query_three, key_three, preferred_element_type=jnp.float32)
    scores = scores * (1.0 / math.sqrt(width))
    allowed = query_image[:, None] == key_image[None, :]
    scores = jnp.where(allowed[None], scores, neg_large)
    newbest = jnp.maximum(best, jnp.max(scores, axis=2))
    weights = jnp.exp(scores - newbest[..., None])
    shrink = jnp.exp(best - newbest)
    total = total * shrink + jnp.sum(weights, axis=2)
    update = jnp.einsum(
        "hqk,khd->hqd",
        weights.astype(jnp.bfloat16),
        value_three,
        preferred_element_type=jnp.float32,
    )
    accum = accum * shrink[..., None] + update
    return (newbest, total, accum)


def on_device(
    queries, key_rows, values, text_keys, text_values, block_image, gate_image, residual, w_out
):
    tok_blk = queries.shape[0]
    ncols = queries.shape[1]
    heads_here = ncols // HD
    blocks_here = tok_blk // BS
    token_image = jnp.repeat(block_image, BS)
    blk_index = lax.axis_index("blk")
    my_blocks = lax.dynamic_slice_in_dim(block_image, blk_index * blocks_here, blocks_here)
    query_image = jnp.repeat(my_blocks, BS)
    text_image = jnp.arange(text_keys.shape[0]) // TEXT
    start_state = (
        jnp.full((heads_here, tok_blk), neg_large, jnp.float32),
        jnp.zeros((heads_here, tok_blk), jnp.float32),
        jnp.zeros((heads_here, tok_blk, HD), jnp.float32),
    )
    query_three = queries.reshape(tok_blk, heads_here, HD)
    running = absorb(start_state, query_three, query_image, text_keys, text_values, text_image)
    fold_running = running
    key_piece = lax.all_gather(key_rows, "blk", axis=0, tiled=True)
    value_piece = lax.all_gather(values, "blk", axis=0, tiled=True)
    length = key_piece.shape[0]

    def advance(state, position):
        begin = position * tok_blk
        key_slab = lax.dynamic_slice_in_dim(key_piece, begin, tok_blk)
        value_slab = lax.dynamic_slice_in_dim(value_piece, begin, tok_blk)
        slab_image = lax.dynamic_slice_in_dim(token_image, begin, tok_blk)
        return (absorb(state, query_three, query_image, key_slab, value_slab, slab_image), None)

    fold_running, unused = lax.scan(
        advance, fold_running, jnp.arange(length // tok_blk, dtype=jnp.int32)
    )
    best, total, accum = fold_running
    attended = (accum / total[..., None]).astype(jnp.bfloat16)
    attended = attended.transpose(1, 0, 2).reshape(tok_blk, ncols)
    tok_dev = tok_blk // lax.axis_size("head")
    mixed = lax.all_to_all(attended, "head", split_axis=0, concat_axis=1, tiled=True)
    projected = jnp.dot(
        mixed, lax.all_gather(w_out, "head", axis=0, tiled=True), preferred_element_type=jnp.float32
    )
    head_index = lax.axis_index("head")
    row_image = lax.dynamic_slice_in_dim(query_image, head_index * tok_dev, tok_dev)
    onehot = (
        row_image[:, None] == jnp.arange(gate_image.shape[0], dtype=jnp.int32)[None, :]
    ).astype(jnp.float32)
    gating = jnp.dot(onehot, gate_image, precision=lax.Precision.HIGHEST)
    return (residual.astype(jnp.float32) + gating * projected).astype(jnp.bfloat16)


def solution(mesh):
    placed = (
        P("blk", "head"),
        P("blk", "head"),
        P("blk", "head"),
        P(None, "head"),
        P(None, "head"),
        P(),
        P(),
        P(("blk", "head"), None),
        P("head", None),
    )
    return jax.shard_map(
        on_device, mesh=mesh, in_specs=placed, out_specs=P(("blk", "head"), None), check_vma=False
    )
```

profile of v0, /device:TPU:0, one launch (start us, length us, event | category | flops | bytes accessed | tf_op | source)
XLA Modules:
  0.0 180.2 jit_solution(2921891639777248629)
XLA Ops:
  6.5 1.8 %copy.33 = bf16[512,256]{0,1:T(8,128)(2,1)} copy(bf16[512,256]{1,0:T(8,128)(2,1)} %param.12) | data formatting | bytes 524288 | tf_op args[1]
  8.5 1.8 copy.34
  15.8 1.8 fusion.21
  17.6 44.9 %all-gather.4.cloned.1.call-done = bf16[4096,256]{0,1:T(8,128)(2,1)} async-done(((bf16[512,256]{0,1:T(8,128)(2,1)}), bf16[4096,256]{0,1:T(8,128)(2,1)}) %all-gather.4.cloned.1.call-update) | async-done | bytes 2097168 | tf_op jit(solution)/shard_map/all_gather | solution.py:60
  62.5 50.6 %all-gather.6.cloned.1.call-done = bf16[4096,256]{0,1:T(8,128)(2,1)} async-done(((bf16[512,256]{0,1:T(8,128)(2,1)}), bf16[4096,256]{0,1:T(8,128)(2,1)}) %all-gather.6.cloned.1.call-update) | async-done | bytes 2097168 | tf_op jit(solution)/shard_map/all_gather | solution.py:61
  113.1 47.1 %while.15 = (s32[]{:T(128)}, f32[4,512]{1,0:T(4,128)S(1)}, f32[4,512]{1,0:T(4,128)S(1)}, f32[4,512,64]{1,2,0:T(8,128)S(1)}, s32[8]{0:T(128)S(1)}, /*index=5*/s32...) while((s32[]{:T(128)}, f32[4,512]{1,0:T(4,128)S(1)}, ...), condition=%wide.region_5.6_spmd.clone, body=%wide.region_2.5_spmd.clone.sunk | while | flops 280498176 | bytes 16656599 | solution.py:71
  114.7 1.1 constant_dynamic-slice_fusion.3
  117.6 1.3 fusion.55
  120.6 1.2 constant_dynamic-slice_fusion.3
  123.7 1.3 fusion.55
  126.6 1.1 constant_dynamic-slice_fusion.3
  129.5 1.3 fusion.55
  135.4 1.3 fusion.55
  138.3 1.1 constant_dynamic-slice_fusion.3
  141.3 1.3 fusion.55
  144.2 1.1 constant_dynamic-slice_fusion.3
  147.1 1.3 fusion.55
  150.1 1.1 constant_dynamic-slice_fusion.3
  153.0 1.3 fusion.55
  155.9 1.1 constant_dynamic-slice_fusion.3
  158.9 1.3 fusion.55
  161.1 3.4 %all-to-all-start = ((bf16[4,128,256]{1,2,0:T(8,128)(2,1)}), bf16[4,128,256]{1,2,0:T(8,128)(2,1)S(1)}, u32[]{:S(2)}, u32[]{:S(2)}) async-start(bf16[4,128,256]{1,2,0:T(8,128)(2,1)} %copy.35), calls=%async_computation | async-start | bytes 524288 | tf_op jit(solution)/shard_map/all_to_all | solution.py:78
  165.0 5.4 %all-to-all-done = bf16[4,128,256]{1,2,0:T(8,128)(2,1)S(1)} async-done(((bf16[4,128,256]{1,2,0:T(8,128)(2,1)}), bf16[4,128,256]{1,2,0:T(8,128)(2,1)S(1)}, u32[]{:S(2)}, u32[]{:S(2)}) %all-to-all-start) | async-done | bytes 262176 | tf_op jit(solution)/shard_map/all_to_all | solution.py:78
  170.4 3.3 %fusion.14 = bf16[128,1536]{1,0:T(8,128)(2,1)} fusion(f32[128,1536]{1,0:T(8,128)S(1)} %fusion.25, bf16[128,1024]{0,1:T(8,128)(2,1)S(1)} %bitcast.63, bf16[1024,1536]{1,0:T(8,128)(2,1)} %all-gather.8.cloned.1.call-done, bf16[128,1536]{1,0:T(8,128)(2,1)S(1)} %copy-done.1), kind=kOutput, calls=%fused_computation.21 | convolution fusion | flops 403439616 | bytes 4980736 | tf_op jit(solution)/shard_map/dot_general | solution.py:79
  (108 shorter events, 30.4 us)
Async XLA Ops:
  6.5 157.9 %copy-start = (f32[2,1536]{1,0:T(2,128)S(1)}, f32[2,1536]{1,0:T(2,128)}, u32[]{:S(2)}) copy-start(f32[2,1536]{1,0:T(2,128)} %param.17) | copy-start | bytes 36868
  6.5 6.0 %copy-start.2 = (bf16[512,256]{1,0:T(8,128)(2,1)S(1)}, bf16[512,256]{1,0:T(8,128)(2,1)}, u32[]{:S(2)}) copy-start(bf16[512,256]{1,0:T(8,128)(2,1)} %param.11) | copy-start | bytes 786436
  6.5 6.2 %copy-start.3 = (bf16[308,256]{1,0:T(8,128)(2,1)S(1)}, bf16[308,256]{1,0:T(8,128)(2,1)}, u32[]{:S(2)}) copy-start(bf16[308,256]{1,0:T(8,128)(2,1)} %param.14) | copy-start | bytes 473092
  6.5 55.9 %all-gather.4.cloned.1.call-start = ((), (), s32[]{:S(2)}) async-start(), calls=%async_computation.1 | async-start | bytes 2359296 | tf_op jit(solution)/shard_map/all_gather | solution.py:60
  8.4 104.7 %all-gather.6.cloned.1.call-start = ((), (), s32[]{:S(2)}) async-start(), calls=%async_computation.2 | async-start | bytes 2359296 | tf_op jit(solution)/shard_map/all_gather | solution.py:61
  10.3 160.2 %all-gather.8.cloned.1.call-start = ((), (), s32[]{:S(2)}) async-start(), calls=%async_computation.3 | async-start | bytes 3932160 | tf_op jit(solution)/shard_map/all_gather | solution.py:80
  13.1 1.9 %copy-start.4 = (bf16[308,256]{1,0:T(8,128)(2,1)S(1)}, bf16[308,256]{1,0:T(8,128)(2,1)}, u32[]{:S(2)}) copy-start(bf16[308,256]{1,0:T(8,128)(2,1)} %param.15) | copy-start | bytes 473092
  160.2 10.3 %copy-start.1 = (bf16[128,1536]{1,0:T(8,128)(2,1)S(1)}, bf16[128,1536]{1,0:T(8,128)(2,1)}, u32[]{:S(2)}) copy-start(bf16[128,1536]{1,0:T(8,128)(2,1)} %param.18) | copy-start | bytes 1179652
  161.1 9.4 %all-to-all-start = ((bf16[4,128,256]{1,2,0:T(8,128)(2,1)}), bf16[4,128,256]{1,2,0:T(8,128)(2,1)S(1)}, u32[]{:S(2)}, u32[]{:S(2)}) async-start(bf16[4,128,256]{1,2,0:T(8,128)(2,1)} %copy.35), calls=%async_computation | async-start | bytes 524288 | tf_op jit(solution)/shard_map/all_to_all | solution.py:78
Sparse Core Ops, SparseCore 0:
  9.4 53.0 all-gather.3
  64.5 48.5 all-gather.5
  114.6 26.6 all-gather.7
where the time goes:
time: 181 us; the launch traced here: 180 us
  waiting for transfers between devices  102 us (56%)
  matrix products  23.7 us (13%)
  local copies, waits for them, and re-layouts  21.8 us (12%)
  between operations  13.2 us (7%)
  other arithmetic  10.6 us (6%)
  loops' own time  5.72 us (3%)
  starting transfers between devices  3.49 us (2%)
    all_gather x1, waiting for transfers between devices, on_device(): value_piece = lax.all_gather(values, 'blk', axis=0, tiled=True)  50.6 us
    all_gather x1, waiting for transfers between devices, on_device(): key_piece = lax.all_gather(key_rows, 'blk', axis=0, tiled=True)  44.9 us
    dot_general x9, matrix products, absorb(): jnp.einsum('hqk,khd->hqd', weights.astype(jnp.bfloat16), value_three, pre...  12 us
    dynamic_slice x8, local copies, waits for them, and re-layouts, advance(): value_slab = lax.dynamic_slice_in_dim(value_piece, begin, tok_blk)  8.77 us
    dot_general x9, matrix products, absorb(): jnp.einsum('qhd,khd->hqk', query_three, key_three, preferred_element_type...  7.99 us
    reduce_sum x9, other arithmetic, absorb(): total = total * shrink + jnp.sum(weights, axis=2)  7.82 us
    another operation x1, loops' own time, on_device(): lax.scan(advance, fold_running, jnp.arange(length // tok_blk, dtype=jnp.i...  5.72 us
    all_to_all x1, waiting for transfers between devices, on_device(): lax.all_to_all(attended, 'head', split_axis=0, concat_axis=1, tiled=True)  5.44 us
  transfers between devices with their start and end apart: 4, of which 3 were waited for; matrix products, arithmetic and copies ran while one was open for 28% of the time, Pallas kernels for 0%

commit v1 on v0

--- a/solution.py
+++ b/solution.py
@@ -3,11 +3,15 @@
 import jax
 import jax.numpy as jnp
 from jax import lax
+from jax.experimental import pallas as pl
+from jax.experimental.pallas import tpu as pltpu
 from jax.sharding import PartitionSpec as P
 
 HD = 64
 TEXT = 154
 BS = 128
+GROUP = 4
+WIDE = 8
 
 
 neg_large = -1e30
@@ -87,6 +91,259 @@
     gating = jnp.dot(onehot, gate_image, precision=lax.Precision.HIGHEST)
     return (residual.astype(jnp.float32) + gating * projected).astype(jnp.bfloat16)
 
+def round_up(count, unit):
+    return -(-count // unit) * unit
+
+
+def pack_kernel(head_ref, q_ref, k_ref, v_ref, tk_ref, tv_ref, send_ref, text_ref):
+    heads = q_ref.shape[1] // HD
+    parts = send_ref.shape[0] // heads
+    rows = q_ref.shape[0]
+    blocks = rows // BS
+    share = BS // parts
+    for h in range(heads):
+        cols = slice(h * HD, (h + 1) * HD)
+        pair = jnp.concatenate([k_ref[:, cols], v_ref[:, cols]], axis=1)
+        for r in range(parts):
+            send_ref[h * parts + r, 0:rows, :] = pair
+            for i in range(blocks // 2):
+                low = i * BS + r * share
+                high = (i + blocks // 2) * BS + r * share
+                send_ref[h * parts + r, rows + i * share : rows + (i + 1) * share, :] = (
+                    jnp.concatenate(
+                        [q_ref[low : low + share, cols], q_ref[high : high + share, cols]], axis=1
+                    )
+                )
+    ntext = tk_ref.shape[0]
+    text_ref[...] = jnp.zeros(text_ref.shape, text_ref.dtype)
+    for h in range(heads):
+
+        @pl.when(head_ref[0] == h)
+        def _():
+            cols = slice(h * HD, (h + 1) * HD)
+            text_ref[0:ntext, :] = jnp.concatenate([tk_ref[:, cols], tv_ref[:, cols]], axis=1)
+
+
+def attend_kernel(
+    image_ref, got_ref, text_ref, out_ref, keys_ref, vals_ref, q_ref, o_ref, start_ref, count_ref, pos_ref
+):
+    nblocks = image_ref.shape[0]
+    images = count_ref.shape[0]
+    sources = got_ref.shape[0]
+    per = nblocks // sources
+    rows = per * BS
+    share = out_ref.shape[1] * 2
+    exponent = math.log2(math.e) / math.sqrt(HD)
+    for i in range(images):
+        count_ref[i] = 0
+
+    def tally(j, carry):
+        image = image_ref[j]
+        count_ref[image] = count_ref[image] + 1
+        return carry
+
+    lax.fori_loop(0, nblocks, tally, 0)
+    begin = jnp.int32(0)
+    for i in range(images):
+        start_ref[i] = begin
+        begin = begin + count_ref[i]
+
+    def place(b, carry):
+        for i in range(per):
+            image = image_ref[b * per + i]
+            spot = start_ref[image]
+            start_ref[image] = spot + 1
+            pos_ref[b * per + i] = spot
+            block = got_ref[b, i * BS : (i + 1) * BS, :]
+            keys_ref[pl.ds(pl.multiple_of(spot * BS, BS), BS), :] = block
+            lane = lax.broadcasted_iota(jnp.int32, block.shape, 1)
+            vals_ref[pl.ds(pl.multiple_of(spot * BS, BS), BS), :] = jnp.where(
+                lane < HD, jnp.ones_like(block), block
+            )
+            half = per // 2
+            qrow = rows + (i % half) * share
+            part = got_ref[b, qrow : qrow + share, :]
+            if i >= half:
+                part = jnp.concatenate([part[:, HD:], part[:, :HD]], axis=1)
+            lane = lax.broadcasted_iota(jnp.int32, part.shape, 1)
+            q_ref[pl.ds(pl.multiple_of(spot * share, share), share), :] = jnp.where(
+                lane < HD, part, jnp.zeros_like(part)
+            )
+        return carry
+
+    lax.fori_loop(0, sources, place, 0)
+    tail = keys_ref.shape[0] - nblocks * BS
+    keys_ref[nblocks * BS :, :] = jnp.zeros((tail, 2 * HD), keys_ref.dtype)
+    vals_ref[nblocks * BS :, :] = jnp.zeros((tail, 2 * HD), vals_ref.dtype)
+    group = GROUP
+    wide = WIDE
+    tile = group * share
+
+    def score(query, slab):
+        return lax.dot_general(
+            query, slab, (((1,), (1,)), ((), ())), preferred_element_type=jnp.float32
+        )
+
+    def one_image(image, carry):
+        count = count_ref[image]
+        first = start_ref[image] - count
+        text_at = image * TEXT
+        shift = text_at % 16
+        window = text_ref[pl.ds(pl.multiple_of(text_at - shift, 16), 256), :]
+        lane = lax.broadcasted_iota(jnp.int32, window.shape, 1)
+        text_vals = jnp.where(lane < HD, jnp.ones_like(window), window)
+        spot = lax.broadcasted_iota(jnp.int32, (1, 256), 1)
+        text_ok = (spot >= shift) & (spot < shift + TEXT)
+
+        def one_tile(t, carry):
+            begin = first + jnp.minimum(t * group, count - group)
+            at = pl.multiple_of(begin * share, share)
+            query = q_ref[pl.ds(at, tile), :]
+            scores = jnp.where(text_ok, score(query, window), neg_large)
+            best = jnp.max(scores, axis=1, keepdims=True)
+            weights = jnp.exp2((scores - best) * exponent).astype(jnp.bfloat16)
+            accum = jnp.dot(weights, text_vals, preferred_element_type=jnp.float32)
+
+            def fold(state, scores, row):
+                best, accum = state
+                newbest = jnp.maximum(best, jnp.max(scores, axis=1, keepdims=True))
+                weights = jnp.exp2((scores - newbest) * exponent).astype(jnp.bfloat16)
+                shrink = jnp.exp2((best - newbest) * exponent)
+                update = jnp.dot(
+                    weights, vals_ref[pl.ds(row, wide * BS), :], preferred_element_type=jnp.float32
+                )
+                return (newbest, accum * shrink + update)
+
+            def full(c, state):
+                row = pl.multiple_of((first + c * wide) * BS, BS)
+                return fold(state, score(query, keys_ref[pl.ds(row, wide * BS), :]), row)
+
+            def rest(state):
+                done = (count // wide) * wide
+                row = pl.multiple_of((first + done) * BS, BS)
+                scores = score(query, keys_ref[pl.ds(row, wide * BS), :])
+                spot = lax.broadcasted_iota(jnp.int32, (1, wide * BS), 1)
+                scores = jnp.where(spot < (count - done) * BS, scores, neg_large)
+                return fold(state, scores, row)
+
+            state = lax.fori_loop(0, count // wide, full, (best, accum))
+            best, accum = lax.cond(count % wide > 0, rest, lambda state: state, state)
+            total = jnp.concatenate([accum[:, HD:], accum[:, :HD]], axis=1)
+            o_ref[pl.ds(at, tile), :] = accum / total
+            return carry
+
+        return lax.fori_loop(0, (count + group - 1) // group, one_tile, carry)
+
+    lax.fori_loop(0, images, one_image, 0)
+
+    def emit(j, carry):
+        at = pl.multiple_of(pos_ref[j] * share, share)
+        half = share // 2
+        block = o_ref[pl.ds(at, share), :].astype(jnp.bfloat16)
+        out_ref[j] = jnp.concatenate([block[:half, HD:], block[half:, HD:]], axis=1)
+        return carry
+
+    lax.fori_loop(0, nblocks, emit, 0)
+
+
+def project_kernel(
+    where_ref, image_ref, got_ref, w0_ref, w1_ref, w2_ref, w3_ref, gate_ref, res_ref, out_ref, mixed_ref
+):
+    groups = mixed_ref.shape[0]
+    heads = mixed_ref.shape[2] // HD
+    half = got_ref.shape[1]
+    parts = got_ref.shape[0] // (groups * heads)
+    for g in range(groups):
+        for r in range(parts):
+            pieces = [got_ref[(h * parts + r) * groups + g] for h in range(heads)]
+            low = r * 2 * half
+            mixed_ref[g, low : low + half, :] = jnp.concatenate(
+                [piece[:, :HD] for piece in pieces], axis=1
+            )
+            mixed_ref[g, low + half : low + 2 * half, :] = jnp.concatenate(
+                [piece[:, HD:] for piece in pieces], axis=1
+            )
+    me = where_ref[0]
+    total = jnp.dot(mixed_ref[me], w0_ref[...], preferred_element_type=jnp.float32)
+    for k, w_ref in ((1, w1_ref), (2, w2_ref), (3, w3_ref)):
+        total += jnp.dot(mixed_ref[me ^ k], w_ref[...], preferred_element_type=jnp.float32)
+    gating = gate_ref[pl.ds(image_ref[where_ref[1]], 1), :]
+    out_ref[...] = (res_ref[...].astype(jnp.float32) + gating * total).astype(jnp.bfloat16)
+
+
+def by_heads(
+    queries, key_rows, values, text_keys, text_values, block_image, gate_image, residual, w_out
+):
+    tok_blk, ncols = queries.shape
+    heads = ncols // HD
+    nblk = lax.axis_size("blk")
+    nhead = lax.axis_size("head")
+    nblocks = block_image.shape[0]
+    images = gate_image.shape[0]
+    parts = nblk // heads
+    share = BS // parts
+    blk = lax.axis_index("blk")
+    head = lax.axis_index("head")
+    smem = pl.BlockSpec(memory_space=pltpu.SMEM)
+    vmem = pl.BlockSpec(memory_space=pltpu.VMEM)
+    packed = tok_blk + tok_blk // parts // 2
+    text_rows = round_up(text_keys.shape[0], 16) + 256
+    bf16 = jnp.bfloat16
+    w1 = lax.ppermute(w_out, "head", [(i, i ^ 1) for i in range(nhead)])
+    w2 = lax.ppermute(w_out, "head", [(i, i ^ 2) for i in range(nhead)])
+    w3 = lax.ppermute(w2, "head", [(i, i ^ 1) for i in range(nhead)])
+    send, text = pl.pallas_call(
+        pack_kernel,
+        out_shape=(
+            jax.ShapeDtypeStruct((nblk, packed, 2 * HD), bf16),
+            jax.ShapeDtypeStruct((text_rows, 2 * HD), bf16),
+        ),
+        in_specs=[smem] + [vmem] * 5,
+        out_specs=(vmem, vmem),
+        name="pack",
+    )((blk // parts).reshape(1), queries, key_rows, values, text_keys, text_values)
+    got = lax.all_to_all(send, "blk", split_axis=0, concat_axis=0, tiled=True)
+    attended = pl.pallas_call(
+        attend_kernel,
+        out_shape=jax.ShapeDtypeStruct((nblocks, share // 2, 2 * HD), bf16),
+        in_specs=[smem, vmem, vmem],
+        out_specs=vmem,
+        scratch_shapes=[
+            pltpu.VMEM(((nblocks + WIDE) * BS, 2 * HD), bf16),
+            pltpu.VMEM(((nblocks + WIDE) * BS, 2 * HD), bf16),
+            pltpu.VMEM((nblocks * share, 2 * HD), bf16),
+            pltpu.VMEM((nblocks * share, 2 * HD), jnp.float32),
+            pltpu.SMEM((images,), jnp.int32),
+            pltpu.SMEM((images,), jnp.int32),
+            pltpu.SMEM((nblocks,), jnp.int32),
+        ],
+        cost_estimate=pl.CostEstimate(
+            flops=8 * HD * nblocks * nblocks * BS * share,
+            transcendentals=nblocks * nblocks * BS * share,
+            bytes_accessed=nblk * packed * 4 * HD,
+        ),
+        name="attend",
+    )(block_image, got, text)
+    mixed = lax.all_to_all(attended, ("blk", "head"), split_axis=0, concat_axis=0, tiled=True)
+    return pl.pallas_call(
+        project_kernel,
+        out_shape=jax.ShapeDtypeStruct(residual.shape, bf16),
+        in_specs=[smem, smem] + [vmem] * 7,
+        out_specs=vmem,
+        scratch_shapes=[pltpu.VMEM((nhead, BS, ncols), bf16)],
+        name="project",
+    )(
+        jnp.stack([head, blk * nhead + head]),
+        block_image,
+        mixed,
+        w_out,
+        w1,
+        w2,
+        w3,
+        gate_image,
+        residual,
+    )
+
 
 def solution(mesh):
     placed = (
@@ -100,6 +357,14 @@
         P(("blk", "head"), None),
         P("head", None),
     )
+    nblk, nhead = mesh.shape["blk"], mesh.shape["head"]
+
+    def step(queries, *others):
+        heads = queries.shape[1] // HD
+        fits = nhead == 4 and nblk % heads == 0 and nblk // heads in (1, 2, 4)
+        fits = fits and queries.shape[0] == nhead * BS
+        return (by_heads if fits else on_device)(queries, *others)
+
     return jax.shard_map(
-        on_device, mesh=mesh, in_specs=placed, out_specs=P(("blk", "head"), None), check_vma=False
-    )
+        step, mesh=mesh, in_specs=placed, out_specs=P(("blk", "head"), None), check_vma=False
+    )

time: 181 us -> 83.6 us (0.46)
  waiting for transfers between devices: 102 us -> 39.7 us
  Pallas kernels: 0 us -> 28.4 us
  matrix products: 23.7 us -> 0 us
  local copies, waits for them, and re-layouts: 21.8 us -> 1.8 us
  between operations: 13.2 us -> 0.03 us
  other arithmetic: 10.6 us -> 0.65 us
  starting transfers between devices: 3.49 us -> 12.7 us
  loops' own time: 5.72 us -> 0 us
    all_gather x3 -> x0, waiting for transfers between devices: 95.5 us -> none  [the longest x1 50.6 us: on_device(): value_piece = lax.all_gather(values, 'blk', axis=0, tiled=True)]
    pallas_call x0 -> x3, Pallas kernels: none -> 28.4 us  [the longest x1 22.2 us: by_heads(): pl.pallas_call(attend_kernel, out_shape=jax.ShapeDtypeStruct((nblocks, sh...]
    dot_general x20 -> x0, matrix products: 23.7 us -> none  [the longest x9 12 us: absorb(): jnp.einsum('hqk,khd->hqd', weights.astype(jnp.bfloat16), value_three, pre...]
    ppermute x0 -> x3, waiting for transfers between devices: none -> 17.5 us  [the longest x1 17.5 us: by_heads(): w2 = lax.ppermute(w_out, 'head', [(i, i ^ 2) for i in range(nhead)])]
    all_to_all x1 -> x2, waiting for transfers between devices: 5.44 us -> 22.2 us  [the longest x1 12.3 us: by_heads(): got = lax.all_to_all(send, 'blk', split_axis=0, concat_axis=0, tiled=True)]
    dynamic_slice x26 -> x0, local copies, waits for them, and re-layouts: 14.9 us -> none  [the longest x8 8.77 us: advance(): value_slab = lax.dynamic_slice_in_dim(value_piece, begin, tok_blk)]
    reduce_sum x9 -> x0, other arithmetic: 7.82 us -> none  [absorb(): total = total * shrink + jnp.sum(weights, axis=2)]
    all_to_all x1 -> x2, starting transfers between devices: 3.41 us -> 11.1 us  [the longest x1 7.45 us: by_heads(): got = lax.all_to_all(send, 'blk', split_axis=0, concat_axis=0, tiled=True)]
  transfers between devices with their start and end apart: 4 -> 5, of which waited for: 3 -> 3; matrix products, arithmetic and copies ran while one was open for 28% -> 1% of each run, Pallas kernels for 0% -> 27%
where the time goes in v1:
time: 83.6 us; the launch traced here: 83.3 us
  waiting for transfers between devices  39.7 us (47%)
  Pallas kernels  28.4 us (34%)
  starting transfers between devices  12.7 us (15%)
  local copies, waits for them, and re-layouts  1.8 us (2%)
    pallas_call x1, Pallas kernels, by_heads(): pl.pallas_call(attend_kernel, out_shape=jax.ShapeDtypeStruct((nblocks, sh...  22.2 us
    ppermute x1, waiting for transfers between devices, by_heads(): w2 = lax.ppermute(w_out, 'head', [(i, i ^ 2) for i in range(nhead)])  17.5 us
    all_to_all x1, waiting for transfers between devices, by_heads(): got = lax.all_to_all(send, 'blk', split_axis=0, concat_axis=0, tiled=True)  12.3 us
    all_to_all x1, waiting for transfers between devices, by_heads(): lax.all_to_all(attended, ('blk', 'head'), split_axis=0, concat_axis=0, ti...  9.91 us
    all_to_all x1, starting transfers between devices, by_heads(): got = lax.all_to_all(send, 'blk', split_axis=0, concat_axis=0, tiled=True)  7.45 us
    all_to_all x1, starting transfers between devices, by_heads(): lax.all_to_all(attended, ('blk', 'head'), split_axis=0, concat_axis=0, ti...  3.65 us
    pallas_call x1, Pallas kernels, by_heads(): pl.pallas_call(project_kernel, out_shape=jax.ShapeDtypeStruct(residual.sh...  3.47 us
    pallas_call x1, Pallas kernels, by_heads(): pl.pallas_call(pack_kernel, out_shape=(jax.ShapeDtypeStruct((nblk, packed...  2.74 us
  transfers between devices with their start and end apart: 5, of which 3 were waited for; matrix products, arithmetic and copies ran while one was open for 1% of the time, Pallas kernels for 27%

profile of v1, /device:TPU:0, one launch (start us, length us, event | category | flops | bytes accessed | tf_op | source)
XLA Modules:
  0.0 83.3 jit_solution(3563738869290386300)
XLA Ops:
  0.0 2.7 %pack.1 = (bf16[8,640,128]{2,1,0:T(8,128)(2,1)}, bf16[576,128]{1,0:T(8,128)(2,1)}) custom-call(s32[1]{0:T(128)} %bitcast.2.head_ref, bf16[512,256]{1,0:T(8,128)(2,1)} %q_ref.1, bf16[512,256]{1,0:T(8,128)(2,1)} %k_ref.1, bf16[512,256]{1,0:T(8,128)(2,1)} %v_ref.1, bf16[308,256]{1,0:T(8,128)(2,1)} %tk_ref.1, bf16[308,256]{1,0:T(8,128)(2,1)} %tv_ref.1), custom_call_target="tpu_custom_call" | custom-call | tf_op jit(solution)/shard_map/pack/pallas_call | solution.py:295
  2.7 0.0 copy-start.2
  2.7 7.4 %all-to-all-start = ((bf16[8,640,128]{2,1,0:T(8,128)(2,1)}), bf16[8,640,128]{2,1,0:T(8,128)(2,1)S(1)}, u32[]{:S(2)}, u32[]{:S(2)}) async-start(bf16[8,640,128]{2,1,0:T(8,128)(2,1)} %get-tuple-element.7), calls=%async_computation | async-start | bytes 2621440 | tf_op jit(solution)/shard_map/all_to_all | solution.py:305
  10.2 0.0 copy-done.2
  10.2 1.6 %collective-permute-start.1 = (bf16[256,1536]{1,0:T(8,128)(2,1)S(1)}, bf16[256,1536]{1,0:T(8,128)(2,1)S(1)}, u32[]{:S(2)}, u32[]{:S(2)}) collective-permute-start(bf16[256,1536]{1,0:T(8,128)(2,1)S(1)} %copy-done.2), channel_id=1, source_target_pairs={{0,2},{1,3},{2,0},{3,1},{4,6},{5,7},{6,4},{7,5},{8,10},{9,11},{10,... | collective-permute-start | bytes 2359304 | tf_op jit(solution)/shard_map/ppermute | solution.py:293
  11.8 0.0 collective-permute-start
  11.8 17.5 %collective-permute-done.1.w2_ref = bf16[256,1536]{1,0:T(8,128)(2,1)S(1)} collective-permute-done((bf16[256,1536]{1,0:T(8,128)(2,1)S(1)}, bf16[256,1536]{1,0:T(8,128)(2,1)S(1)}, u32[]{:S(2)}, u32[]{:S(2)}) %collective-permute-start.1) | collective-permute-done | bytes 786464 | tf_op jit(solution)/shard_map/ppermute | solution.py:293
  29.3 0.0 copy-start.3
  29.3 0.0 collective-permute-start.2
  29.3 12.3 %all-to-all-done.got_ref = bf16[8,640,128]{2,1,0:T(8,128)(2,1)S(1)} async-done(((bf16[8,640,128]{2,1,0:T(8,128)(2,1)}), bf16[8,640,128]{2,1,0:T(8,128)(2,1)S(1)}, u32[]{:S(2)}, u32[]{:S(2)}) %all-to-all-start) | async-done | bytes 1310752 | tf_op jit(solution)/shard_map/all_to_all | solution.py:305
  41.6 0.0 copy-start
  41.6 1.1 %copy-done = bf16[8,640,128]{2,1,0:T(8,128)(2,1)} copy-done((bf16[8,640,128]{2,1,0:T(8,128)(2,1)}, bf16[8,640,128]{2,1,0:T(8,128)(2,1)S(1)}, u32[]{:S(2)}) %copy-start) | copy-done | bytes 1310744
  42.7 22.2 %attend.1 = bf16[32,32,128]{2,1,0:T(8,128)(2,1)} custom-call(s32[32]{0:T(128)} %image_ref.3, bf16[8,640,128]{2,1,0:T(8,128)(2,1)} %copy-done, bf16[576,128]{1,0:T(8,128)(2,1)} %get-tuple-element.8.text_ref), custom_call_target="tpu_custom_call" | custom-call | flops 4294967296 | bytes 1310720 | tf_op jit(solution)/shard_map/attend/pallas_call | solution.py:306
  64.9 0.0 copy-done.3
  64.9 3.7 %all-to-all-start.1 = ((bf16[32,32,128]{2,1,0:T(8,128)(2,1)}), bf16[32,32,128]{2,1,0:T(8,128)(2,1)S(1)}, u32[]{:S(2)}, u32[]{:S(2)}) async-start(bf16[32,32,128]{2,1,0:T(8,128)(2,1)} %attend.1), calls=%async_computation.1 | async-start | bytes 524288 | tf_op jit(solution)/shard_map/all_to_all | solution.py:327
  68.5 0.6 pad_add_fusion.where_ref
  69.2 0.0 collective-permute-done.w1_ref
  69.2 0.0 collective-permute-done.2.w3_ref
  69.2 9.9 %all-to-all-done.1.got_ref = bf16[32,32,128]{2,1,0:T(8,128)(2,1)S(1)} async-done(((bf16[32,32,128]{2,1,0:T(8,128)(2,1)}), bf16[32,32,128]{2,1,0:T(8,128)(2,1)S(1)}, u32[]{:S(2)}, u32[]{:S(2)}) %all-to-all-start.1) | async-done | bytes 262176 | tf_op jit(solution)/shard_map/all_to_all | solution.py:327
  79.1 0.0 copy-start.1
  79.1 0.7 copy-done.1
  79.8 3.5 %project.1 = bf16[128,1536]{1,0:T(8,128)(2,1)} custom-call(s32[2]{0:T(128)} %pad_add_fusion.where_ref, s32[32]{0:T(128)} %image_ref.3, bf16[32,32,128]{2,1,0:T(8,128)(2,1)} %copy-done.1, bf16[256,1536]{1,0:T(8,128)(2,1)} %w0_ref.1, bf16[256,1536]{1,0:T(8,128)(2,1)} %collective-permute-done.w1_ref, bf16[256,1536]{1,0:T(8,128)(2,1)} %copy-done.3, ...), custom_call_target="tpu_custom_call" | custom-call | tf_op jit(solution)/shard_map/project/pallas_call | solution.py:328
Async XLA Ops:
  2.7 7.5 %copy-start.2 = (bf16[256,1536]{1,0:T(8,128)(2,1)S(1)}, bf16[256,1536]{1,0:T(8,128)(2,1)}, u32[]{:S(2)}) copy-start(bf16[256,1536]{1,0:T(8,128)(2,1)} %w0_ref.1) | copy-start | bytes 2359300
  2.7 38.8 %all-to-all-start = ((bf16[8,640,128]{2,1,0:T(8,128)(2,1)}), bf16[8,640,128]{2,1,0:T(8,128)(2,1)S(1)}, u32[]{:S(2)}, u32[]{:S(2)}) async-start(bf16[8,640,128]{2,1,0:T(8,128)(2,1)} %get-tuple-element.7), calls=%async_computation | async-start | bytes 2621440 | tf_op jit(solution)/shard_map/all_to_all | solution.py:305
  10.2 19.1 %collective-permute-start.1 = (bf16[256,1536]{1,0:T(8,128)(2,1)S(1)}, bf16[256,1536]{1,0:T(8,128)(2,1)S(1)}, u32[]{:S(2)}, u32[]{:S(2)}) collective-permute-start(bf16[256,1536]{1,0:T(8,128)(2,1)S(1)} %copy-done.2), channel_id=1, source_target_pairs={{0,2},{1,3},{2,0},{3,1},{4,6},{5,7},{6,4},{7,5},{8,10},{9,11},{10,... | collective-permute-start | bytes 2359304 | tf_op jit(solution)/shard_map/ppermute | solution.py:293
  11.8 57.4 %collective-permute-start = (bf16[256,1536]{1,0:T(8,128)(2,1)S(1)}, bf16[256,1536]{1,0:T(8,128)(2,1)}, u32[]{:S(2)}, u32[]{:S(2)}) collective-permute-start(bf16[256,1536]{1,0:T(8,128)(2,1)S(1)} %copy-done.2), channel_id=1, source_target_pairs={{0,1},{1,0},{2,3},{3,2},{4,5},{5,4},{6,7},{7,6},{8,9},{9,8},{10,11... | collective-permute-start | bytes 2359304 | tf_op jit(solution)/shard_map/ppermute | solution.py:292
  29.3 35.6 %copy-start.3 = (bf16[256,1536]{1,0:T(8,128)(2,1)}, bf16[256,1536]{1,0:T(8,128)(2,1)S(1)}, u32[]{:S(2)}) copy-start(bf16[256,1536]{1,0:T(8,128)(2,1)S(1)} %collective-permute-done.1.w2_ref) | copy-start | bytes 2359300
  29.3 39.9 %collective-permute-start.2 = (bf16[256,1536]{1,0:T(8,128)(2,1)S(1)}, bf16[256,1536]{1,0:T(8,128)(2,1)}, u32[]{:S(2)}, u32[]{:S(2)}) collective-permute-start(bf16[256,1536]{1,0:T(8,128)(2,1)S(1)} %collective-permute-done.1.w2_ref), channel_id=1, source_target_pairs={{0,1},{1,0},{2,3},{3,2},{4,5},{5,4},{6,7},{7,6},{8,9},{9,8},{10,11... | collective-permute-start | bytes 2359304 | tf_op jit(solution)/shard_map/ppermute | solution.py:294
  41.6 1.1 %copy-start = (bf16[8,640,128]{2,1,0:T(8,128)(2,1)}, bf16[8,640,128]{2,1,0:T(8,128)(2,1)S(1)}, u32[]{:S(2)}) copy-start(bf16[8,640,128]{2,1,0:T(8,128)(2,1)S(1)} %all-to-all-done.got_ref) | copy-start | bytes 3932164
  64.9 14.2 %all-to-all-start.1 = ((bf16[32,32,128]{2,1,0:T(8,128)(2,1)}), bf16[32,32,128]{2,1,0:T(8,128)(2,1)S(1)}, u32[]{:S(2)}, u32[]{:S(2)}) async-start(bf16[32,32,128]{2,1,0:T(8,128)(2,1)} %attend.1), calls=%async_computation.1 | async-start | bytes 524288 | tf_op jit(solution)/shard_map/all_to_all | solution.py:327
  79.1 0.7 copy-start.1
